TPU v7x, 32 devices: a whole 2x2x4 slice. The times are simulated.
32 devices in a mesh: expert: 8 (over y, x, core), dp: 4 (over z).
Axes of the slice: x: 2, y: 2, z: 4, core: 2. Of those that a mesh axis runs over, the one named last changes fastest.
Arguments:
- tokens: bfloat16 [512, 2048], P(('expert', 'dp')), may hold values from -6 to 6
- out_grad: bfloat16 [512, 2048], P(('expert', 'dp')), may hold values from -6 to 6
- routes: int32 [512, 8], P(('expert', 'dp')), may hold values from 0 to 15, all different within a row; in each aligned block of 16 rows (0 to 15, 16 to 31, ...) at most 16 rows name the same one
- route_gates: float32 [512, 8], P(('expert', 'dp')), may hold values from 0.05 to 0.5
- w_gate: bfloat16 [16, 2048, 384], P('expert'), may hold values from -0.125 to 0.125
- w_up: bfloat16 [16, 2048, 384], P('expert'), may hold values from -0.125 to 0.125
- w_down: bfloat16 [16, 384, 2048], P('expert'), may hold values from -0.3125 to 0.3125
Outputs:
- token_grad: bfloat16 [512, 2048], P(('expert', 'dp'))
- down_grad: float32 [384, 16, 2048], P('dp', 'expert')
Inputs may be any that keep to these rules, and one draw needn't show every extreme that they name: `routes`: each row names 8 different experts. Among the 16 tokens of one device no expert is named more than 16 times, a bound that some block reaches.
All inputs are finite; a program needn't handle non-finite values.
Results may differ from a plain program's by a relative error of at most 0.014.
Values may be sent and summed in bfloat16 or wider, within the bound.
A program may use at most 64 MiB of HBM per device.

v0:
```python
import jax
import jax.numpy as jnp
from jax import lax
from jax.sharding import PartitionSpec as P


def gate_up(arrived, w_gate, w_up):
    gate_pre = jnp.einsum("erd,edf->erf", arrived, w_gate, preferred_element_type=jnp.float32)
    up_pre = jnp.einsum("erd,edf->erf", arrived, w_up, preferred_element_type=jnp.float32)
    return (gate_pre, up_pre)


def shards(tokens, out_grad, routes, route_gates, w_gate, w_up, w_down):
    tok_count, model_width = tokens.shape
    top_count = routes.shape[1]
    local_experts = w_gate.shape[0]
    groups = lax.axis_size("expert")
    experts = local_experts * groups
    slot_count = 2 * tok_count * top_count // experts
    flat_routes = routes.reshape(-1)
    onehot = (flat_routes[:, None] == jnp.arange(experts, dtype=jnp.int32)[None, :]).astype(
        jnp.int32
    )
    slot_rank = jnp.sum(onehot * (jnp.cumsum(onehot, axis=0) - onehot), axis=1)
    slot_index = flat_routes * slot_count + slot_rank
    placement = slot_index[None, :] == jnp.arange(experts * slot_count, dtype=jnp.int32)[:, None]
    route_place = placement.astype(jnp.bfloat16)
    token_place = jnp.sum(
        placement.reshape(experts * slot_count, tok_count, top_count).astype(jnp.float32), axis=2
    ).astype(jnp.bfloat16)
    send_inputs = (
        jnp.dot(token_place, tokens, preferred_element_type=jnp.float32)
        .astype(jnp.bfloat16)
        .reshape(experts, slot_count, model_width)
    )
    scaled = (
        (route_gates[:, :, None] * out_grad[:, None, :].astype(jnp.float32))
        .astype(jnp.bfloat16)
        .reshape(tok_count * top_count, model_width)
    )
    send_grads = (
        jnp.dot(route_place, scaled, preferred_element_type=jnp.float32)
        .astype(jnp.bfloat16)
        .reshape(experts, slot_count, model_width)
    )
    arrived, arrived_grad = (
        lax.all_to_all(send_inputs, "expert", split_axis=0, concat_axis=1, tiled=True),
        lax.all_to_all(send_grads, "expert", split_axis=0, concat_axis=1, tiled=True),
    )
    gate_pre, up_pre = gate_up(arrived, w_gate, w_up)
    sigmoid_gate = jax.nn.sigmoid(gate_pre)
    silu_gate = gate_pre * sigmoid_gate
    hidden = (silu_gate * up_pre).astype(jnp.bfloat16)
    hidden_grad = jnp.einsum(
        "erd,efd->erf", arrived_grad, w_down, preferred_element_type=jnp.float32
    )
    gate_grad = (
        hidden_grad * up_pre * (sigmoid_gate + gate_pre * sigmoid_gate * (1.0 - sigmoid_gate))
    ).astype(jnp.bfloat16)
    up_grad = (hidden_grad * silu_gate).astype(jnp.bfloat16)
    row_grads = (
        jnp.einsum("erf,edf->erd", gate_grad, w_gate, preferred_element_type=jnp.float32)
        + jnp.einsum("erf,edf->erd", up_grad, w_up, preferred_element_type=jnp.float32)
    ).astype(jnp.bfloat16)
    returned = lax.all_to_all(row_grads, "expert", split_axis=1, concat_axis=0, tiled=True)
    token_grad = lax.dot_general(
        token_place,
        returned.reshape(experts * slot_count, model_width),
        (((0,), (0,)), ((), ())),
        preferred_element_type=jnp.float32,
    ).astype(jnp.bfloat16)
    hidden_units = hidden.shape[2]
    share_rows = hidden_units // lax.axis_size("dp")
    partial_grad = jnp.einsum(
        "erf,erd->fed", hidden, arrived_grad, preferred_element_type=jnp.float32
    ).astype(jnp.bfloat16)
    total_grad = lax.psum(partial_grad, "dp").astype(jnp.float32)
    first_row = lax.axis_index("dp") * share_rows
    down_grad = lax.dynamic_slice_in_dim(total_grad, first_row, share_rows, 0)
    return (token_grad, down_grad)


def solution(mesh):
    placed = (
        P(("expert", "dp"), None),
        P(("expert", "dp"), None),
        P(("expert", "dp"), None),
        P(("expert", "dp"), None),
        P("expert", None, None),
        P("expert", None, None),
        P("expert", None, None),
    )
    return jax.shard_map(
        shards,
        mesh=mesh,
        in_specs=placed,
        out_specs=(P(("expert", "dp"), None), P("dp", "expert", None)),
        check_vma=False,
    )
```

profile of v0, /device:TPU:0, one launch (start us, length us, event | category | flops | bytes accessed | tf_op | source)
XLA Modules:
  0.0 193.7 jit_solution(11863418635343941623)
XLA Ops:
  7.2 0.9 copy.42
  8.7 0.9 convert_element_type.51
  9.5 0.8 copy.44
  10.4 1.5 convolution_convert_fusion.1
  11.8 5.2 %all-to-all-start = ((bf16[16,16,2048]{2,1,0:T(8,128)(2,1)}), bf16[16,16,2048]{2,1,0:T(8,128)(2,1)}, u32[]{:S(2)}, u32[]{:S(2)}) async-start(bf16[16,16,2048]{2,1,0:T(8,128)(2,1)} %bitcast.38), calls=%async_computation | async-start | bytes 2097152 | tf_op jit(solution)/shard_map/all_to_all | solution.py:48
  17.3 1.5 convolution_convert_fusion.2
  18.7 13.8 %all-to-all-done = bf16[16,16,2048]{2,1,0:T(8,128)(2,1)} async-done(((bf16[16,16,2048]{2,1,0:T(8,128)(2,1)}), bf16[16,16,2048]{2,1,0:T(8,128)(2,1)}, u32[]{:S(2)}, u32[]{:S(2)}) %all-to-all-start) | async-done | bytes 1048608 | tf_op jit(solution)/shard_map/all_to_all | solution.py:48
  32.5 4.2 %all-to-all-start.1 = ((bf16[16,16,2048]{2,1,0:T(8,128)(2,1)}), bf16[16,16,2048]{2,1,0:T(8,128)(2,1)}, u32[]{:S(2)}, u32[]{:S(2)}) async-start(bf16[16,16,2048]{2,1,0:T(8,128)(2,1)} %bitcast.39), calls=%async_computation.1 | async-start | bytes 2097152 | tf_op jit(solution)/shard_map/all_to_all | solution.py:47
  36.8 2.3 %copy.45 = bf16[8,2,16,2048]{3,2,0,1:T(8,128)(2,1)} copy(bf16[8,2,16,2048]{3,2,1,0:T(8,128)(2,1)} %bitcast.2) | data formatting | bytes 2097152 | tf_op jit(solution)/shard_map/all_to_all | solution.py:48
  39.1 13.0 %all-to-all-done.1 = bf16[16,16,2048]{2,1,0:T(8,128)(2,1)} async-done(((bf16[16,16,2048]{2,1,0:T(8,128)(2,1)}), bf16[16,16,2048]{2,1,0:T(8,128)(2,1)}, u32[]{:S(2)}, u32[]{:S(2)}) %all-to-all-start.1) | async-done | bytes 1048608 | tf_op jit(solution)/shard_map/all_to_all | solution.py:47
  52.2 1.5 copy.46
  55.9 2.7 %fusion = bf16[384,2,2048]{0,2,1:T(8,128)(2,1)} fusion(bf16[2,128,2048]{2,1,0:T(8,128)(2,1)S(1)} %bitcast.35, f32[2,128,384]{2,1,0:T(8,128)S(1)} %fusion.18, f32[2,128,384]{2,1,0:T(8,128)S(1)} %fusion.19), kind=kOutput, calls=%fused_computation.1 | convolution fusion | flops 404815872 | bytes 4980736 | tf_op jit(solution)/shard_map/erf,erd->fed/dot_general | solution.py:74
  58.7 3.3 %fusion.17 = f32[2,128,384]{2,1,0:T(8,128)S(1)} fusion(bf16[2,128,2048]{2,1,0:T(8,128)(2,1)} %bitcast.34, bf16[2,384,2048]{2,1,0:T(8,128)(2,1)} %param.13), kind=kOutput, calls=%fused_computation.31 | convolution fusion | flops 402653184 | bytes 4587520 | tf_op jit(solution)/shard_map/erd,efd->erf/dot_general | solution.py:54
  62.0 1.1 fusion.7
  63.1 0.8 copy-done.2
  63.9 1.1 fusion.1
  65.0 2.0 %copy.47 = bf16[2,128,2048]{2,0,1:T(2,128)(2,1)} copy(bf16[2,128,2048]{2,1,0:T(8,128)(2,1)S(1)} %fusion.1) | data formatting | bytes 2097152 | tf_op jit(solution)/shard_map/convert_element_type | solution.py:64
  67.1 4.2 %all-to-all-start.2 = ((bf16[2,128,2048]{2,0,1:T(2,128)(2,1)}), bf16[2,128,2048]{2,0,1:T(2,128)(2,1)}, u32[]{:S(2)}, u32[]{:S(2)}) async-start(bf16[2,128,2048]{2,0,1:T(2,128)(2,1)} %copy.47), calls=%async_computation.2 | async-start | bytes 2097152 | tf_op jit(solution)/shard_map/all_to_all | solution.py:65
  71.3 15.4 %all-to-all-done.2 = bf16[2,128,2048]{2,0,1:T(2,128)(2,1)} async-done(((bf16[2,128,2048]{2,0,1:T(2,128)(2,1)}), bf16[2,128,2048]{2,0,1:T(2,128)(2,1)}, u32[]{:S(2)}, u32[]{:S(2)}) %all-to-all-start.2) | async-done | bytes 1048608 | tf_op jit(solution)/shard_map/all_to_all | solution.py:65
  86.7 1.6 copy.48
  88.4 0.9 convolution_convert_fusion.3
  89.3 90.4 %all-reduce.2.cloned.1.call-done = bf16[384,2,2048]{0,2,1:T(8,128)(2,1)} async-done(((bf16[384,2,2048]{0,2,1:T(8,128)(2,1)}), bf16[384,2,2048]{0,2,1:T(8,128)(2,1)}) %all-reduce.2.cloned.1.call-update) | async-done | bytes 3145744 | tf_op jit(solution)/shard_map/psum | solution.py:77
  179.7 3.3 %dynamic-slice_convert_fusion = f32[96,2,2048]{0,2,1:T(8,128)} fusion(bf16[384,2,2048]{0,2,1:T(8,128)(2,1)} %all-reduce.2.cloned.1.call-done, s32[]{:T(128)S(6)} %select_n.3), kind=kLoop, calls=%fused_computation.7 | loop fusion | flops 393216 | bytes 2359300 | tf_op jit(solution)/shard_map/convert_element_type | solution.py:77
  183.0 3.9 %copy.51 = f32[96,2,2048]{2,1,0:T(2,128)} copy(f32[96,2,2048]{0,2,1:T(8,128)} %dynamic-slice_convert_fusion) | data formatting | bytes 3145728
  (27 shorter events, 3.2 us)
Async XLA Ops:
  7.2 46.5 %copy-start = (bf16[2,2048,384]{2,1,0:T(8,128)(2,1)S(1)}, bf16[2,2048,384]{2,1,0:T(8,128)(2,1)}, u32[]{:S(2)}) copy-start(bf16[2,2048,384]{2,1,0:T(8,128)(2,1)} %param.11) | copy-start | bytes 9437188
  7.2 10.1 %copy-start.6 = (bf16[16,2048]{1,0:T(8,128)(2,1)S(1)}, bf16[16,2048]{1,0:T(8,128)(2,1)}, u32[]{:S(2)}) copy-start(bf16[16,2048]{1,0:T(8,128)(2,1)} %param.7) | copy-start | bytes 196612
  11.8 20.7 %all-to-all-start = ((bf16[16,16,2048]{2,1,0:T(8,128)(2,1)}), bf16[16,16,2048]{2,1,0:T(8,128)(2,1)}, u32[]{:S(2)}, u32[]{:S(2)}) async-start(bf16[16,16,2048]{2,1,0:T(8,128)(2,1)} %bitcast.38), calls=%async_computation | async-start | bytes 2097152 | tf_op jit(solution)/shard_map/all_to_all | solution.py:48
  32.5 19.6 %all-to-all-start.1 = ((bf16[16,16,2048]{2,1,0:T(8,128)(2,1)}), bf16[16,16,2048]{2,1,0:T(8,128)(2,1)}, u32[]{:S(2)}, u32[]{:S(2)}) async-start(bf16[16,16,2048]{2,1,0:T(8,128)(2,1)} %bitcast.39), calls=%async_computation.1 | async-start | bytes 2097152 | tf_op jit(solution)/shard_map/all_to_all | solution.py:47
  36.8 142.9 %all-reduce.2.cloned.1.call-start = ((), (), s32[]{:S(2)}) async-start(), calls=%async_computation.3 | async-start | bytes 6291456 | tf_op jit(solution)/shard_map/psum | solution.py:77
  52.2 2.3 %copy-start.1 = (bf16[2,2048,384]{2,1,0:T(8,128)(2,1)S(1)}, bf16[2,2048,384]{2,1,0:T(8,128)(2,1)}, u32[]{:S(2)}) copy-start(bf16[2,2048,384]{2,1,0:T(8,128)(2,1)} %param.12) | copy-start | bytes 9437188
  54.4 1.5 copy-start.3
  55.1 0.8 copy-start.4
  58.6 3.3 %copy-start.5 = (f32[2,128,384]{2,1,0:T(8,128)S(1)}, f32[2,128,384]{2,1,0:T(8,128)}, u32[]{:S(2)}) copy-start(f32[2,128,384]{2,1,0:T(8,128)} %copy-done.4) | copy-start | bytes 1179652
  62.0 1.9 copy-start.2
  67.1 19.6 %all-to-all-start.2 = ((bf16[2,128,2048]{2,0,1:T(2,128)(2,1)}), bf16[2,128,2048]{2,0,1:T(2,128)(2,1)}, u32[]{:S(2)}, u32[]{:S(2)}) async-start(bf16[2,128,2048]{2,0,1:T(2,128)(2,1)} %copy.47), calls=%async_computation.2 | async-start | bytes 2097152 | tf_op jit(solution)/shard_map/all_to_all | solution.py:65
Sparse Core Ops, SparseCore 0:
  58.8 120.8 all-reduce.1
where the time goes:
time: 194 us
  waiting for transfers between devices  133 us (69%)
  local copies, waits for them, and re-layouts  14.9 us (8%)
  between operations  14.2 us (7%)
  starting transfers between devices  13.7 us (7%)
  matrix products  13.5 us (7%)
  other arithmetic  4.72 us (2%)
    psum x1, waiting for transfers between devices, shards(): total_grad = lax.psum(partial_grad, 'dp').astype(jnp.float32)  90.4 us
    all_to_all x1, waiting for transfers between devices, shards(): lax.all_to_all(row_grads, 'expert', split_axis=1, concat_axis=0, tiled=True)  15.4 us
    all_to_all x1, waiting for transfers between devices, shards(): lax.all_to_all(send_grads, 'expert', split_axis=0, concat_axis=1, tiled=T...  13.8 us
    all_to_all x1, waiting for transfers between devices, shards(): lax.all_to_all(send_inputs, 'expert', split_axis=0, concat_axis=1, tiled=...  13 us
    unnamed x17, local copies, waits for them, and re-layouts  7.11 us
    all_to_all x1, starting transfers between devices, shards(): lax.all_to_all(send_grads, 'expert', split_axis=0, concat_axis=1, tiled=T...  5.2 us
    all_to_all x1, starting transfers between devices, shards(): lax.all_to_all(row_grads, 'expert', split_axis=1, concat_axis=0, tiled=True)  4.25 us
    all_to_all x1, starting transfers between devices, shards(): lax.all_to_all(send_inputs, 'expert', split_axis=0, concat_axis=1, tiled=...  4.24 us
  transfers between devices with their start and end apart: 4, of which 4 were waited for; matrix products, arithmetic and copies ran while one was open for 7% of the time, Pallas kernels for 0%

commit v1 on v0

--- a/solution.py
+++ b/solution.py
@@ -74,7 +74,7 @@
     partial_grad = jnp.einsum(
         "erf,erd->fed", hidden, arrived_grad, preferred_element_type=jnp.float32
     ).astype(jnp.bfloat16)
-    total_grad = lax.psum(partial_grad, "dp").astype(jnp.float32)
+    total_grad = jnp.sum(lax.all_gather(partial_grad, "dp"), axis=0).astype(jnp.float32)
     first_row = lax.axis_index("dp") * share_rows
     down_grad = lax.dynamic_slice_in_dim(total_grad, first_row, share_rows, 0)
     return (token_grad, down_grad)

time: 194 us -> 382 us (1.97)
  waiting for transfers between devices: 133 us -> 230 us
  other arithmetic: 4.72 us -> 72.9 us
  local copies, waits for them, and re-layouts: 14.9 us -> 36.4 us
    all_gather x0 -> x1, waiting for transfers between devices: none -> 188 us  [shards(): lax.all_gather(partial_grad, 'dp')]
    psum x1 -> x0, waiting for transfers between devices: 90.4 us -> none  [shards(): total_grad = lax.psum(partial_grad, 'dp').astype(jnp.float32)]
    reduce_sum x0 -> x1, other arithmetic: none -> 68.1 us  [shards(): jnp.sum(lax.all_gather(partial_grad, 'dp'), axis=0).astype(jnp.float32)]
    all_gather x0 -> x1, local copies, waits for them, and re-layouts: none -> 21.6 us  [shards(): lax.all_gather(partial_grad, 'dp')]
  transfers between devices with their start and end apart: 4 -> 4, of which waited for: 4 -> 4; matrix products, arithmetic and copies ran while one was open for 7% -> 4% of each run, Pallas kernels for 0% -> 0%
where the time goes in v1:
time: 382 us; the launch traced here: 381 us
  waiting for transfers between devices  230 us (60%)
  other arithmetic  72.9 us (19%)
  local copies, waits for them, and re-layouts  36.4 us (10%)
  between operations  14.2 us (4%)
  starting transfers between devices  13.9 us (4%)
  matrix products  13.5 us (4%)
    all_gather x1, waiting for transfers between devices, shards(): lax.all_gather(partial_grad, 'dp')  188 us
    reduce_sum x1, other arithmetic, shards(): jnp.sum(lax.all_gather(partial_grad, 'dp'), axis=0).astype(jnp.float32)  68.1 us
    all_gather x1, local copies, waits for them, and re-layouts, shards(): lax.all_gather(partial_grad, 'dp')  21.6 us
    all_to_all x1, waiting for transfers between devices, shards(): lax.all_to_all(row_grads, 'expert', split_axis=1, concat_axis=0, tiled=True)  15.2 us
    all_to_all x1, waiting for transfers between devices, shards(): lax.all_to_all(send_grads, 'expert', split_axis=0, concat_axis=1, tiled=T...  13.8 us
    all_to_all x1, waiting for transfers between devices, shards(): lax.all_to_all(send_inputs, 'expert', split_axis=0, concat_axis=1, tiled=...  13 us
  transfers between devices with their start and end apart: 4, of which 4 were waited for; matrix products, arithmetic and copies ran while one was open for 4% of the time, Pallas kernels for 0%

profile of v1, /device:TPU:0, one launch (start us, length us, event | category | flops | bytes accessed | tf_op | source)
XLA Modules:
  0.0 380.5 jit_solution(10172495662815579167)
XLA Ops:
  7.2 0.9 copy.40
  8.7 0.9 convert_element_type.53
  10.4 1.5 convolution_convert_fusion.1
  11.8 5.2 %all-to-all-start = ((bf16[16,16,2048]{2,1,0:T(8,128)(2,1)}), bf16[16,16,2048]{2,1,0:T(8,128)(2,1)}, u32[]{:S(2)}, u32[]{:S(2)}) async-start(bf16[16,16,2048]{2,1,0:T(8,128)(2,1)} %bitcast.40), calls=%async_computation | async-start | bytes 2097152 | tf_op jit(solution)/shard_map/all_to_all | solution.py:48
  17.3 1.4 convolution_convert_fusion.2
  18.7 13.8 %all-to-all-done = bf16[16,16,2048]{2,1,0:T(8,128)(2,1)} async-done(((bf16[16,16,2048]{2,1,0:T(8,128)(2,1)}), bf16[16,16,2048]{2,1,0:T(8,128)(2,1)}, u32[]{:S(2)}, u32[]{:S(2)}) %all-to-all-start) | async-done | bytes 1048608 | tf_op jit(solution)/shard_map/all_to_all | solution.py:48
  32.5 4.2 %all-to-all-start.1 = ((bf16[16,16,2048]{2,1,0:T(8,128)(2,1)}), bf16[16,16,2048]{2,1,0:T(8,128)(2,1)}, u32[]{:S(2)}, u32[]{:S(2)}) async-start(bf16[16,16,2048]{2,1,0:T(8,128)(2,1)} %bitcast.41), calls=%async_computation.1 | async-start | bytes 2097152 | tf_op jit(solution)/shard_map/all_to_all | solution.py:47
  36.8 2.3 copy.43
  39.1 13.0 %all-to-all-done.1 = bf16[16,16,2048]{2,1,0:T(8,128)(2,1)} async-done(((bf16[16,16,2048]{2,1,0:T(8,128)(2,1)}), bf16[16,16,2048]{2,1,0:T(8,128)(2,1)}, u32[]{:S(2)}, u32[]{:S(2)}) %all-to-all-start.1) | async-done | bytes 1048608 | tf_op jit(solution)/shard_map/all_to_all | solution.py:47
  52.2 1.5 copy.44
  55.9 2.7 fusion
  58.6 3.3 fusion.17
  62.0 1.1 fusion.7
  63.8 1.1 fusion.1
  65.0 2.0 copy.45
  67.0 4.4 %all-to-all-start.2 = ((bf16[2,128,2048]{2,0,1:T(2,128)(2,1)}), bf16[2,128,2048]{2,0,1:T(2,128)(2,1)}, u32[]{:S(2)}, u32[]{:S(2)}) async-start(bf16[2,128,2048]{2,0,1:T(2,128)(2,1)} %copy.45), calls=%async_computation.2 | async-start | bytes 2097152 | tf_op jit(solution)/shard_map/all_to_all | solution.py:65
  71.5 15.2 %all-to-all-done.2 = bf16[2,128,2048]{2,0,1:T(2,128)(2,1)} async-done(((bf16[2,128,2048]{2,0,1:T(2,128)(2,1)}), bf16[2,128,2048]{2,0,1:T(2,128)(2,1)}, u32[]{:S(2)}, u32[]{:S(2)}) %all-to-all-start.2) | async-done | bytes 1048608 | tf_op jit(solution)/shard_map/all_to_all | solution.py:65
  86.7 1.6 copy.46
  88.4 0.9 convolution_convert_fusion.3
  89.3 187.5 %all-gather.3.cloned.1.call-done = bf16[1536,2,2048]{0,2,1:T(8,128)(2,1)} async-done(((bf16[384,2,2048]{0,2,1:T(8,128)(2,1)}), bf16[1536,2,2048]{0,2,1:T(8,128)(2,1)}) %all-gather.3.cloned.1.call-update) | async-done | bytes 12582928 | tf_op jit(solution)/shard_map/all_gather | solution.py:77
  276.8 21.6 %reshape.44 = bf16[4,384,2,2048]{1,0,3,2:T(4,128)(2,1)} reshape(bf16[1536,2,2048]{0,2,1:T(8,128)(2,1)} %all-gather.3.cloned.1.call-done) | data formatting | bytes 25165824 | tf_op jit(solution)/shard_map/all_gather | solution.py:77
  298.4 68.1 %reduce_sum.35 = bf16[384,2,2048]{0,2,1:T(8,128)(2,1)} reduce(bf16[4,384,2,2048]{1,0,3,2:T(4,128)(2,1)} %reshape.44, bf16[]{:T(256)} %constant.18.clone.1), dimensions={0}, to_apply=%region_3.4 | reduce | flops 4718592 | bytes 15728642 | tf_op jit(solution)/shard_map/reduce_sum | solution.py:77
  366.5 3.3 dynamic-slice_convert_fusion
  369.8 3.9 %copy.49 = f32[96,2,2048]{2,1,0:T(2,128)} copy(f32[96,2,2048]{0,2,1:T(8,128)} %dynamic-slice_convert_fusion) | data formatting | bytes 3145728
  (29 shorter events, 4.7 us)
Async XLA Ops:
  7.2 46.5 %copy-start = (bf16[2,2048,384]{2,1,0:T(8,128)(2,1)S(1)}, bf16[2,2048,384]{2,1,0:T(8,128)(2,1)}, u32[]{:S(2)}) copy-start(bf16[2,2048,384]{2,1,0:T(8,128)(2,1)} %param.11) | copy-start | bytes 9437188
  7.2 10.1 %copy-start.6 = (bf16[16,2048]{1,0:T(8,128)(2,1)S(1)}, bf16[16,2048]{1,0:T(8,128)(2,1)}, u32[]{:S(2)}) copy-start(bf16[16,2048]{1,0:T(8,128)(2,1)} %param.7) | copy-start | bytes 196612
  11.8 20.7 %all-to-all-start = ((bf16[16,16,2048]{2,1,0:T(8,128)(2,1)}), bf16[16,16,2048]{2,1,0:T(8,128)(2,1)}, u32[]{:S(2)}, u32[]{:S(2)}) async-start(bf16[16,16,2048]{2,1,0:T(8,128)(2,1)} %bitcast.40), calls=%async_computation | async-start | bytes 2097152 | tf_op jit(solution)/shard_map/all_to_all | solution.py:48
  32.5 19.6 %all-to-all-start.1 = ((bf16[16,16,2048]{2,1,0:T(8,128)(2,1)}), bf16[16,16,2048]{2,1,0:T(8,128)(2,1)}, u32[]{:S(2)}, u32[]{:S(2)}) async-start(bf16[16,16,2048]{2,1,0:T(8,128)(2,1)} %bitcast.41), calls=%async_computation.1 | async-start | bytes 2097152 | tf_op jit(solution)/shard_map/all_to_all | solution.py:47
  36.8 240.0 %all-gather.3.cloned.1.call-start = ((), (), s32[]{:S(2)}) async-start(), calls=%async_computation.3 | async-start | bytes 15728640 | tf_op jit(solution)/shard_map/all_gather | solution.py:77
  52.2 2.3 copy-start.1
  54.4 1.5 copy-start.3
  55.2 0.7 copy-start.4
  58.6 3.3 copy-start.5
  61.9 1.9 copy-start.2
  67.0 19.7 %all-to-all-start.2 = ((bf16[2,128,2048]{2,0,1:T(2,128)(2,1)}), bf16[2,128,2048]{2,0,1:T(2,128)(2,1)}, u32[]{:S(2)}, u32[]{:S(2)}) async-start(bf16[2,128,2048]{2,0,1:T(2,128)(2,1)} %copy.45), calls=%async_computation.2 | async-start | bytes 2097152 | tf_op jit(solution)/shard_map/all_to_all | solution.py:65
Sparse Core Ops, SparseCore 0:
  58.7 218.0 all-gather.2
